TPU v7x, 32 devices: a whole 2x2x4 slice. The times are simulated.
32 devices in a mesh: seq: 8 (over y, x, core), tp: 4 (over z).
Axes of the slice: x: 2, y: 2, z: 4, core: 2. Of those that a mesh axis runs over, the one named last changes fastest.
Arguments:
- layer_in: bfloat16 [2, 2048, 2048], P(None, 'seq'), may hold values from -6 to 6
- attn_gain: float32 [2048], replicated, may hold values from 0.1 to 1.9
- query_down: bfloat16 [2048, 1024], replicated, may hold values from -0.125 to 0.125
- latent_gain: float32 [1024], replicated, may hold values from 0.1 to 1.9
- query_up: bfloat16 [1024, 4096], P(None, 'tp'), may hold values from -0.1875 to 0.1875
- key_value: bfloat16 [2048, 512], replicated, may hold values from -0.125 to 0.125
- attn_out: bfloat16 [4096, 2048], P('tp'), may hold values from -1.5 to 1.5
- ffn_gain: float32 [2048], replicated, may hold values from 0.1 to 1.9
- gate_proj: bfloat16 [2048, 5632], P(None, 'tp'), may hold values from -0.125 to 0.125
- up_proj: bfloat16 [2048, 5632], P(None, 'tp'), may hold values from -0.125 to 0.125
- down_proj: bfloat16 [5632, 2048], P('tp'), may hold values from -0.078125 to 0.078125
- out_grad: bfloat16 [2, 2048, 2048], P(None, 'seq'), may hold values from -6 to 6
- doc_lengths: int32 [2, 8], replicated, may hold values from 1 to 1536, 2048 in all within a row
Outputs:
- layer_out: bfloat16 [2, 2048, 2048], P(None, 'seq')
- input_grad: bfloat16 [2, 2048, 2048], P(None, 'seq')
- attn_gain_grad: float32 [2048], P('seq')
- query_down_grad: float32 [2048, 1024], P('seq')
- latent_gain_grad: float32 [1024], P('seq')
- query_up_grad: float32 [1024, 4096], P('seq', 'tp')
- key_value_grad: float32 [2048, 512], P('seq')
- attn_out_grad: float32 [4096, 2048], P('tp', 'seq')
- ffn_gain_grad: float32 [2048], P('seq')
- gate_proj_grad: float32 [2048, 5632], P('seq', 'tp')
- up_proj_grad: float32 [2048, 5632], P('seq', 'tp')
- down_proj_grad: float32 [5632, 2048], P('tp', 'seq')
Inputs may be any that keep to these rules, and one draw needn't show every extreme that they name: `doc_lengths`: in each row the 8 lengths add up to 2048, and the longest is exactly 1536.
All inputs are finite; a program needn't handle non-finite values.
Results may differ from a plain program's by a relative error of at most 0.019.
Values may be sent and summed in bfloat16 or wider, within the bound.
No kernel may reach another device: no remote copies, remote signals or barrier semaphores. Data moves between devices by JAX's collectives and lax.ppermute only.
A program may use at most 256 MiB of HBM per device.

v0:
```python
import jax
import jax.numpy as jnp
from jax import lax
from jax.sharding import PartitionSpec as P

HD = 256
EPS = 1e-05
ROPE_BASE = 10000.0
NEG_FILL = -1e30


def matmul(left, right):
    return jnp.dot(left, right, preferred_element_type=jnp.float32)


def dot_rows(left, right):
    return lax.dot_general(
        left, right, (((0,), (0,)), ((), ())), preferred_element_type=jnp.float32
    )


def dot_cols(left, right):
    return lax.dot_general(
        left, right, (((1,), (1,)), ((), ())), preferred_element_type=jnp.float32
    )


def rms_forward(values, gain_vec):
    inv_rms = lax.rsqrt(jnp.mean(values * values, axis=-1, keepdims=True) + EPS)
    unit_rows = values * inv_rms
    return (unit_rows * gain_vec, unit_rows, inv_rms)


def rms_backward(grad_out, unit_rows, inv_rms, gain_vec):
    scaled = grad_out * gain_vec
    return inv_rms * (scaled - unit_rows * jnp.mean(scaled * unit_rows, axis=-1, keepdims=True))


def doc_layout(lengths, places):
    doc_ends = jnp.cumsum(lengths)
    starts = doc_ends - lengths
    owners = jnp.sum((places[:, None] >= doc_ends[None, :]).astype(jnp.int32), axis=1)
    member = owners[:, None] == jnp.arange(lengths.shape[0], dtype=jnp.int32)[None, :]
    inner_pos = places - jnp.sum(jnp.where(member, starts[None, :], 0), axis=1)
    return (owners, inner_pos)


def rotate(values, inner_pos, direction):
    half_dim = values.shape[-1] // 2
    frequency = ROPE_BASE ** (-jnp.arange(half_dim, dtype=jnp.float32) / half_dim)
    angles = inner_pos.astype(jnp.float32)[..., None] * frequency
    for padding_axis in range(values.ndim - 1 - angles.ndim + 1):
        angles = angles[..., None, :]
    cosine = jnp.cos(angles)
    sine_part = jnp.sin(angles) * direction
    front_half = values[..., :half_dim]
    back_half = values[..., half_dim:]
    return jnp.concatenate(
        [front_half * cosine - back_half * sine_part, back_half * cosine + front_half * sine_part],
        axis=-1,
    )


def key_scores(query_rows, key_piece, query_owner, query_place, lengths):
    count = key_piece.shape[1]
    key_places = jnp.arange(count, dtype=jnp.int32)

    def owner_rows(lengths_row):
        return doc_layout(lengths_row, key_places)[0]

    key_owner = jax.vmap(owner_rows)(lengths)
    scores = jnp.einsum(
        "rqd,rkd->rqk", query_rows, key_piece[..., :HD], preferred_element_type=jnp.float32
    ) * HD ** (-0.5)
    allowed = (query_owner[:, :, None] == key_owner[:, None, :]) & (
        key_places[None, None, :] <= query_place[None, :, None]
    )
    return (jnp.where(allowed, scores, NEG_FILL), allowed)


def forward_fold(carry, key_piece, query_rows, query_owner, query_place, lengths):
    row_peak, row_total, context = carry
    scores, allowed = key_scores(query_rows, key_piece, query_owner, query_place, lengths)
    new_peak = jnp.maximum(row_peak, jnp.max(scores, axis=-1))
    expo_vals = jnp.where(allowed, jnp.exp(scores - new_peak[..., None]), 0.0)
    row_total = jnp.sum(expo_vals, axis=-1)
    context = jnp.einsum(
        "rqk,rkd->rqd",
        expo_vals.astype(jnp.bfloat16),
        key_piece[..., HD:],
        preferred_element_type=jnp.float32,
    )
    return (new_peak, row_total, context)


def backward_fold(
    key_piece, query_rows, query_owner, query_place, lengths, log_total, context_rows, row_delta
):
    scores, allowed = key_scores(query_rows, key_piece, query_owner, query_place, lengths)
    probs = jnp.where(allowed, jnp.exp(scores - log_total[..., None]), 0.0)
    dprobs = jnp.einsum(
        "rqd,rkd->rqk", context_rows, key_piece[..., HD:], preferred_element_type=jnp.float32
    )
    dscores = (probs * (dprobs - row_delta[..., None])).astype(jnp.bfloat16)
    dquery = jnp.einsum(
        "rqk,rkd->rqd", dscores, key_piece[..., :HD], preferred_element_type=jnp.float32
    )
    dkeys = jnp.einsum(
        "rqk,rqd->rkd", dscores, query_rows, preferred_element_type=jnp.float32
    ) * HD ** (-0.5)
    dvalues = jnp.einsum(
        "rqk,rqd->rkd", probs.astype(jnp.bfloat16), context_rows, preferred_element_type=jnp.float32
    )
    update = jnp.concatenate([dkeys, dvalues], axis=-1)
    return (dquery, update)


def key_backward(kv_delta, inner_pos):
    turned = rotate(kv_delta[..., :HD], inner_pos, -1.0)
    return jnp.concatenate([turned, kv_delta[..., HD:]], axis=-1).astype(jnp.bfloat16)


def shards(
    layer_in,
    attn_gain,
    query_down,
    latent_gain,
    query_up,
    key_value,
    attn_out,
    ffn_gain,
    gate_proj,
    up_proj,
    down_proj,
    out_grad,
    doc_lengths,
):
    row_count, row_tokens, model_dim = layer_in.shape
    shard_index = lax.axis_index("seq")
    local_heads = query_up.shape[1] // HD
    tokens = row_count * row_tokens
    query_count = local_heads * row_tokens
    places = shard_index * row_tokens + jnp.arange(row_tokens, dtype=jnp.int32)

    def layout_row(lengths_row):
        return doc_layout(lengths_row, places)

    owners, inner_pos = jax.vmap(layout_row)(doc_lengths)
    stream = layer_in.astype(jnp.float32).reshape(tokens, model_dim)
    normed_full, unit_first, inv_first = rms_forward(stream, attn_gain)
    normed = normed_full.astype(jnp.bfloat16)
    latent = matmul(normed, query_down)
    latent_full, unit_latent, inv_latent = rms_forward(latent, latent_gain)
    latent_norm = latent_full.astype(jnp.bfloat16)
    raw_query = matmul(latent_norm, query_up).reshape(row_count, row_tokens, local_heads, HD)
    queries = rotate(raw_query, inner_pos, 1.0).astype(jnp.bfloat16)
    query_rows = queries.transpose(0, 2, 1, 3).reshape(row_count, query_count, HD)
    query_owner = jnp.tile(owners, (1, local_heads))
    query_place = jnp.tile(places, local_heads)
    kv_proj = matmul(normed, key_value).reshape(row_count, row_tokens, 2 * HD)
    key_part = rotate(kv_proj[..., :HD], inner_pos, 1.0)
    kv_shard = jnp.concatenate([key_part, kv_proj[..., HD:]], axis=-1).astype(jnp.bfloat16)
    start_carry = (
        jnp.full((row_count, query_count), NEG_FILL, jnp.float32),
        jnp.zeros((row_count, query_count), jnp.float32),
        jnp.zeros((row_count, query_count, HD), jnp.float32),
    )
    row_peak, row_total, context = forward_fold(
        start_carry,
        lax.all_gather(kv_shard, "seq", axis=1, tiled=True),
        query_rows,
        query_owner,
        query_place,
        doc_lengths,
    )
    context = context / row_total[..., None]
    log_total = row_peak + jnp.log(row_total)
    context_low = context.astype(jnp.bfloat16)
    context_flat = (
        context_low.reshape(row_count, local_heads, row_tokens, HD)
        .transpose(0, 2, 1, 3)
        .reshape(tokens, local_heads * HD)
    )
    attn_total = lax.psum(matmul(context_flat, attn_out), "tp")
    middle = stream + attn_total
    second_full, unit_second, inv_second = rms_forward(middle, ffn_gain)
    second_norm = second_full.astype(jnp.bfloat16)
    gate_act = matmul(second_norm, gate_proj)
    up_act = matmul(second_norm, up_proj)
    sigmoid_gate = jax.nn.sigmoid(gate_act)
    swish_gate = gate_act * sigmoid_gate
    hidden = (swish_gate * up_act).astype(jnp.bfloat16)
    ffn_total = lax.psum(matmul(hidden, down_proj), "tp")
    layer_out = (middle + ffn_total).astype(jnp.bfloat16).reshape(row_count, row_tokens, model_dim)
    grad_low = out_grad.reshape(tokens, model_dim)
    grad_full = grad_low.astype(jnp.float32)
    down_grad = dot_rows(hidden, grad_low)
    dhidden = dot_cols(grad_low, down_proj)
    gate_delta = (dhidden * up_act * sigmoid_gate * (1.0 + gate_act * (1.0 - sigmoid_gate))).astype(
        jnp.bfloat16
    )
    up_delta = (dhidden * swish_gate).astype(jnp.bfloat16)
    gate_grad = dot_rows(second_norm, gate_delta)
    upproj_grad = dot_rows(second_norm, up_delta)
    second_delta = lax.psum(dot_cols(gate_delta, gate_proj) + dot_cols(up_delta, up_proj), "tp")
    middle_delta = grad_full + rms_backward(second_delta, unit_second, inv_second, ffn_gain)
    middle_low = middle_delta.astype(jnp.bfloat16)
    mixer_grad = dot_rows(context_flat, middle_low)
    column_grads = (
        lax.psum_scatter(mixer_grad, "seq", scatter_dimension=1, tiled=True),
        lax.psum_scatter(down_grad, "seq", scatter_dimension=1, tiled=True),
    )
    context_delta = dot_cols(middle_low, attn_out).astype(jnp.bfloat16)
    context_rows = (
        context_delta.reshape(row_count, row_tokens, local_heads, HD)
        .transpose(0, 2, 1, 3)
        .reshape(row_count, query_count, HD)
    )
    row_delta = jnp.sum(context_rows.astype(jnp.float32) * context, axis=-1)
    dquery, key_deltas = backward_fold(
        lax.all_gather(kv_shard, "seq", axis=1, tiled=True),
        query_rows,
        query_owner,
        query_place,
        doc_lengths,
        log_total,
        context_rows,
        row_delta,
    )
    kv_part = lax.psum_scatter(key_deltas, "seq", scatter_dimension=1, tiled=True)
    dquery = dquery * HD ** (-0.5)
    query_delta = dquery.reshape(row_count, local_heads, row_tokens, HD).transpose(0, 2, 1, 3)
    query_low = (
        rotate(query_delta, inner_pos, -1.0).astype(jnp.bfloat16).reshape(tokens, local_heads * HD)
    )
    expand_grad = dot_rows(latent_norm, query_low)
    latent_part = dot_cols(query_low, query_up)
    latent_delta, kv_summed = lax.psum((latent_part, kv_part), "tp")
    kv_low = key_backward(kv_summed, inner_pos).reshape(tokens, 2 * HD)
    latent_back = rms_backward(latent_delta, unit_latent, inv_latent, latent_gain)
    latent_low = latent_back.astype(jnp.bfloat16)
    normed_delta = dot_cols(latent_low, query_down) + dot_cols(kv_low, key_value)
    input_grad = (
        (middle_delta + rms_backward(normed_delta, unit_first, inv_first, attn_gain))
        .astype(jnp.bfloat16)
        .reshape(row_count, row_tokens, model_dim)
    )
    gain_first = jnp.sum(normed_delta * unit_first, axis=0)
    gain_latent = jnp.sum(latent_delta * unit_latent, axis=0)
    gain_second = jnp.sum(second_delta * unit_second, axis=0)
    compress_grad = dot_rows(normed, latent_low)
    shared_grad = dot_rows(normed, kv_low)
    row_grads = (
        lax.psum_scatter(gain_first, "seq", scatter_dimension=0, tiled=True),
        lax.psum_scatter(compress_grad, "seq", scatter_dimension=0, tiled=True),
        lax.psum_scatter(gain_latent, "seq", scatter_dimension=0, tiled=True),
        lax.psum_scatter(expand_grad, "seq", scatter_dimension=0, tiled=True),
        lax.psum_scatter(shared_grad, "seq", scatter_dimension=0, tiled=True),
        lax.psum_scatter(gain_second, "seq", scatter_dimension=0, tiled=True),
        lax.psum_scatter(gate_grad, "seq", scatter_dimension=0, tiled=True),
        lax.psum_scatter(upproj_grad, "seq", scatter_dimension=0, tiled=True),
    )
    return (
        layer_out,
        input_grad,
        row_grads[0],
        row_grads[1],
        row_grads[2],
        row_grads[3],
        row_grads[4],
        column_grads[0],
        row_grads[5],
        row_grads[6],
        row_grads[7],
        column_grads[1],
    )


def solution(mesh):
    return jax.shard_map(
        shards,
        mesh=mesh,
        in_specs=(
            P(None, "seq", None),
            P(),
            P(),
            P(),
            P(None, "tp"),
            P(),
            P("tp", None),
            P(),
            P(None, "tp"),
            P(None, "tp"),
            P("tp", None),
            P(None, "seq", None),
            P(),
        ),
        out_specs=(
            P(None, "seq", None),
            P(None, "seq", None),
            P("seq"),
            P("seq", None),
            P("seq"),
            P("seq", "tp"),
            P("seq", None),
            P("tp", "seq"),
            P("seq"),
            P("seq", "tp"),
            P("seq", "tp"),
            P("tp", "seq"),
        ),
        check_vma=False,
    )
```

profile of v0, /device:TPU:0, one launch (start us, length us, event | category | flops | bytes accessed | tf_op | source)
XLA Modules:
  0.0 1362.6 jit_solution(8796911887741906710)
XLA Ops:
  11.2 2.9 fusion.24
  23.6 2.6 fusion.63
  26.2 3.5 reshape.210
  33.6 2.7 iota_compare_fusion
  36.3 20.2 %all-gather.2.cloned.1.call-done = bf16[2,2048,512]{2,1,0:T(8,128)(2,1)} async-done(((bf16[2,256,512]{2,1,0:T(8,128)(2,1)}), bf16[2,2048,512]{2,1,0:T(8,128)(2,1)}) %all-gather.2.cloned.1.call-update) | async-done | bytes 4194320 | tf_op jit(solution)/shard_map/all_gather | solution.py:170
  56.5 7.5 fusion.64
  64.6 6.1 fusion
  70.8 8.6 fusion.40
  82.8 4.4 fusion.65
  87.3 155.1 %all-reduce.9.cloned.1.call-done = f32[512,2048]{1,0:T(8,128)} async-done(((f32[512,2048]{1,0:T(8,128)}), f32[512,2048]{1,0:T(8,128)}) %all-reduce.9.cloned.1.call-update) | async-done | bytes 4194320 | tf_op jit(solution)/shard_map/psum | solution.py:184
  242.3 3.5 multiply_reduce_fusion.2
  246.3 10.1 fusion.67
  256.5 5.0 fusion.66
  261.5 8.1 multiply_convert_fusion.2
  269.6 4.9 fusion.69
  274.6 5.1 convolution_add_fusion.1
  280.4 153.5 %all-reduce.11.cloned.1.call-done = f32[512,2048]{1,0:T(8,128)} async-done(((f32[512,2048]{1,0:T(8,128)}), f32[512,2048]{1,0:T(8,128)}) %all-reduce.11.cloned.1.call-update) | async-done | bytes 4194320 | tf_op jit(solution)/shard_map/psum | solution.py:205
  433.9 4.6 multiply_reduce_fusion
  439.8 2.8 multiply_add_fusion
  444.6 3.3 convolution_convert_fusion
  452.5 12.0 fusion.3
  464.5 13.9 %multiply_convert_fusion = bf16[2,1024,2048]{2,1,0:T(8,128)(2,1)} fusion(f32[2,1024,2048]{2,1,0:T(8,128)} %copy-done.9, f32[2,1024]{1,0:T(2,128)S(1)} %multiply_reduce_fusion.5, f32[2,1024]{1,0:T(2,128)S(1)} %log_add_fusion, s32[2,2048]{1,0:T(2,128)S(1)} %convert_reduce_fusion, s32[2,1024]{1,0:T(2,128)S(1)} %bitcast.132, ...), kind=kOutput, calls=%fused_computation | convolution fusion | flops 2176843776 | bytes 30449664 | tf_op jit(solution)/shard_map/rqd,rkd->rqk/dot_general | solution.py:101
  478.4 6.9 convolution_multiply_fusion
  485.4 4.6 pad_maximum_fusion
  491.3 8.2 fusion.68
  499.6 7.2 fusion.34
  509.7 2.6 fusion.70
  512.3 48.1 %reduce-scatter.9.cloned.1.call-done = f32[2,256,512]{2,1,0:T(8,128)} async-done(((f32[2,2048,512]{2,1,0:T(8,128)}), f32[2,256,512]{2,1,0:T(8,128)}) %reduce-scatter.9.cloned.1.call-update) | async-done | bytes 1048592 | tf_op jit(solution)/shard_map/reduce_scatter | solution.py:230
  560.5 5.1 fusion.62
  566.8 8.0 fusion.37
  576.1 9.0 fusion.75
  586.5 7.7 fusion.74
  595.6 7.8 fusion.73
  603.4 217.7 %all-reduce.13.cloned.1.call-done = (f32[512,2048]{1,0:T(8,128)}, f32[512,1024]{1,0:T(8,128)}, f32[2,256,512]{2,1,0:T(8,128)}) async-done(((f32[512,2048]{1,0:T(8,128)}, f32[512,1024]{1,0:T(8,128)}, f32[2,256,512]{2,1,0:T(8,128)}), (f32[512,2048]{1,0:T(8,128)}, f32[512,1024]{1,0:T(8,128)}, f32[2,256,512]{2,1,0:T(8,128)})) %all-reduce.13.cloned.1.call-update) | async-done | bytes 7340048 | tf_op jit(solution)/shard_map/psum | solution.py:193
  825.0 4.9 fusion.56
  830.3 4.0 multiply_reduce_fusion.3
  835.4 5.7 fusion.72
  843.7 4.7 fusion.71
  848.5 3.8 fusion.19
  852.3 24.3 %all-reduce.3 = (f32[2048]{0:T(1024)S(1)}, f32[1024]{0:T(1024)S(1)}, f32[2048]{0:T(1024)S(1)}) all-reduce(f32[2048]{0:T(1024)S(1)} %get-tuple-element.14, f32[1024]{0:T(1024)S(1)} %copy-done.42, f32[2048]{0:T(1024)S(1)} %get-tuple-element.12), channel_id=3, replica_groups=mesh['seq'=8,'tp'=4] {'seq'}, use_global_device_ids=true, to_apply=%region_20.21.clone | all-reduce | flops 5120 | bytes 40960
  878.4 5.6 add_convert_fusion
  886.2 2.4 fusion.18
  888.6 62.4 %reduce-scatter.17.cloned.1.call-done = f32[1024,256]{1,0:T(8,128)} async-done(((f32[1024,2048]{1,0:T(8,128)}), f32[1024,256]{1,0:T(8,128)}) %reduce-scatter.17.cloned.1.call-update) | async-done | bytes 1048592 | tf_op jit(solution)/shard_map/reduce_scatter | solution.py:210
  951.0 91.3 %reduce-scatter.23.cloned.1.call-done = f32[1408,256]{1,0:T(8,128)} async-done(((f32[1408,2048]{1,0:T(8,128)}), f32[1408,256]{1,0:T(8,128)}) %reduce-scatter.23.cloned.1.call-update) | async-done | bytes 1441808 | tf_op jit(solution)/shard_map/reduce_scatter | solution.py:211
  1042.3 91.3 %reduce-scatter.21.cloned.1.call-done = f32[256,1408]{1,0:T(8,128)} async-done(((f32[2048,1408]{1,0:T(8,128)}), f32[256,1408]{1,0:T(8,128)}) %reduce-scatter.21.cloned.1.call-update) | async-done | bytes 1441808 | tf_op jit(solution)/shard_map/reduce_scatter | solution.py:261
  1133.6 91.1 %reduce-scatter.19.cloned.1.call-done = f32[256,1408]{1,0:T(8,128)} async-done(((f32[2048,1408]{1,0:T(8,128)}), f32[256,1408]{1,0:T(8,128)}) %reduce-scatter.19.cloned.1.call-update) | async-done | bytes 1441808 | tf_op jit(solution)/shard_map/reduce_scatter | solution.py:260
  1224.7 55.6 %reduce-scatter.15.cloned.1.call-done = f32[256,512]{1,0:T(8,128)} async-done(((f32[2048,512]{1,0:T(8,128)}), f32[256,512]{1,0:T(8,128)}) %reduce-scatter.15.cloned.1.call-update) | async-done | bytes 524304 | tf_op jit(solution)/shard_map/reduce_scatter | solution.py:258
  1280.4 75.2 %reduce-scatter.11.cloned.1.call-done = f32[256,1024]{1,0:T(8,128)} async-done(((f32[2048,1024]{1,0:T(8,128)}), f32[256,1024]{1,0:T(8,128)}) %reduce-scatter.11.cloned.1.call-update) | async-done | bytes 1048592 | tf_op jit(solution)/shard_map/reduce_scatter | solution.py:255
  (201 shorter events, 50.6 us)
Async XLA Ops:
  7.2 49.3 %all-gather.2.cloned.1.call-start = ((), (), s32[]{:S(2)}) async-start(), calls=%async_computation.8 | async-start | bytes 4718592 | tf_op jit(solution)/shard_map/all_gather | solution.py:170
  7.3 6.9 copy-start.43
  9.1 5.1 copy-start.40
  11.2 5.8 copy-start.33
  16.0 13.7 %copy-start.20 = (f32[2,256,128]{2,1,0:T(8,128)}, f32[2,256,128]{2,1,0:T(8,128)S(1)}, u32[]{:S(2)}) copy-start(f32[2,256,128]{2,1,0:T(8,128)S(1)} %get-tuple-element.41) | copy-start | bytes 786436
  16.9 225.4 %all-reduce.9.cloned.1.call-start = ((), (), s32[]{:S(2)}) async-start(), calls=%async_computation.9 | async-start | bytes 8388608 | tf_op jit(solution)/shard_map/psum | solution.py:184
  17.0 5.3 copy-start.37
  56.5 8.1 copy-start.14
  64.0 6.7 copy-start.9
  87.2 158.6 %copy-start.30 = (f32[2048]{0:T(1024)S(1)}, f32[2048]{0:T(1024)}, u32[]{:S(2)}) copy-start(f32[2048]{0:T(1024)} %param.20) | copy-start | bytes 24580
  87.2 346.6 %all-reduce.11.cloned.1.call-start = ((), (), s32[]{:S(2)}) async-start(), calls=%async_computation.10 | async-start | bytes 8388608 | tf_op jit(solution)/shard_map/psum | solution.py:205
  245.8 10.6 copy-start.1
  245.9 10.6 slice-start
  246.3 10.1 copy-start.22
  246.3 10.1 slice-start.1
  246.3 15.2 %slice-start.4 = ((s8[5767168]{0:T(1024)(128)(4,1)}), s8[4194304]{0:T(1024)(128)(4,1)S(1)}, s32[]{:S(2)}) async-start(s8[5767168]{0:T(1024)(128)(4,1)} %bitcast.141), calls=%async_computation.24 | async-start | bytes 8388608
  256.4 5.1 copy-start.23
  256.4 5.0 slice-start.5
  256.5 18.1 %slice-start.2 = ((s8[5767168]{0:T(1024)(128)(4,1)}), s8[4194304]{0:T(1024)(128)(4,1)S(1)}, s32[]{:S(2)}) async-start(s8[5767168]{0:T(1024)(128)(4,1)} %bitcast.139), calls=%async_computation.22 | async-start | bytes 8388608
  261.5 13.1 slice-start.3
  269.6 5.0 copy-start.55
  279.7 280.7 %reduce-scatter.9.cloned.1.call-start = ((), (), s32[]{:S(2)}) async-start(), calls=%async_computation.11 | async-start | bytes 9437184 | tf_op jit(solution)/shard_map/reduce_scatter | solution.py:230
  433.9 5.9 copy-start.10
  439.8 4.8 copy-start.46
  464.5 13.9 %copy-start.25 = (bf16[2,4,256,256]{3,2,1,0:T(8,128)(2,1)S(1)}, bf16[2,4,256,256]{3,2,1,0:T(8,128)(2,1)}, u32[]{:S(2)}) copy-start(bf16[2,4,256,256]{3,2,1,0:T(8,128)(2,1)} %copy.48) | copy-start | bytes 3145732
  478.4 7.0 copy-start.17
  490.0 331.1 %all-reduce.13.cloned.1.call-start = ((), (), s32[]{:S(2)}) async-start(), calls=%async_computation.19 | async-start | bytes 14680064 | tf_op jit(solution)/shard_map/psum | solution.py:193
  491.3 8.3 copy-start.48
  512.3 48.2 %copy-start.29 = (f32[1024]{0:T(1024)S(1)}, f32[1024]{0:T(1024)}, u32[]{:S(2)}) copy-start(f32[1024]{0:T(1024)} %param.16) | copy-start | bytes 12292
  512.3 48.2 %copy-start.32 = (f32[512]{0:T(512)S(1)}, f32[512]{0:T(512)}, u32[]{:S(2)}) copy-start(f32[512]{0:T(512)} %copy-done.31) | copy-start | bytes 6148
  560.4 328.2 %reduce-scatter.13.cloned.1.call-start = ((), (), s32[]{:S(2)}) async-start(), calls=%async_computation.13 | async-start | bytes 4718592 | tf_op jit(solution)/shard_map/reduce_scatter | solution.py:257
  565.6 385.5 %reduce-scatter.17.cloned.1.call-start = ((), (), s32[]{:S(2)}) async-start(), calls=%async_computation.15 | async-start | bytes 9437184 | tf_op jit(solution)/shard_map/reduce_scatter | solution.py:210
  574.8 467.5 %reduce-scatter.23.cloned.1.call-start = ((), (), s32[]{:S(2)}) async-start(), calls=%async_computation.18 | async-start | bytes 12976128 | tf_op jit(solution)/shard_map/reduce_scatter | solution.py:211
  585.1 548.5 %reduce-scatter.21.cloned.1.call-start = ((), (), s32[]{:S(2)}) async-start(), calls=%async_computation.17 | async-start | bytes 12976128 | tf_op jit(solution)/shard_map/reduce_scatter | solution.py:261
  594.2 630.5 %reduce-scatter.19.cloned.1.call-start = ((), (), s32[]{:S(2)}) async-start(), calls=%async_computation.16 | async-start | bytes 12976128 | tf_op jit(solution)/shard_map/reduce_scatter | solution.py:260
  603.3 218.8 %copy-start.41 = (f32[2,256]{1,0:T(2,128)S(1)}, f32[2,256]{1,0:T(2,128)}, u32[]{:S(2)}) copy-start(f32[2,256]{1,0:T(2,128)} %copy-done.40) | copy-start | bytes 6148
  603.3 218.8 %copy-start.44 = (f32[128]{0:T(128)S(1)}, f32[128]{0:T(128)}, u32[]{:S(2)}) copy-start(f32[128]{0:T(128)} %copy-done.43) | copy-start | bytes 1540
  603.4 677.0 %reduce-scatter.15.cloned.1.call-start = ((), (), s32[]{:S(2)}) async-start(), calls=%async_computation.14 | async-start | bytes 4718592 | tf_op jit(solution)/shard_map/reduce_scatter | solution.py:258
  830.0 525.6 %reduce-scatter.11.cloned.1.call-start = ((), (), s32[]{:S(2)}) async-start(), calls=%async_computation.12 | async-start | bytes 9437184 | tf_op jit(solution)/shard_map/reduce_scatter | solution.py:255
  830.3 5.2 copy-start.12
  843.7 4.8 copy-start.5
  843.7 4.8 copy-start.27
  843.7 4.8 copy-start.34
  843.7 4.8 copy-start.38
  848.5 35.5 %copy-start.39 = (f32[1,2,2,128]{3,1,2,0:T(2,128)S(1)}, f32[1,2,2,128]{3,1,2,0:T(2,128)}, u32[]{:S(2)}) copy-start(f32[1,2,2,128]{3,1,2,0:T(2,128)} %copy-done.37) | copy-start | bytes 6148
  878.4 5.6 copy-start.4
  878.4 5.6 copy-start.6
  878.4 7.8 copy-start.16
  (27 other events, 58.8 us)
Sparse Core Ops, SparseCore 0:
  17.1 39.4 all-gather.1
  87.3 154.9 all-reduce.8
  279.8 153.9 all-reduce.10
  490.1 70.2 reduce-scatter.8
  563.6 257.4 all-reduce.12
  825.2 50.4 reduce-scatter.12
  879.8 71.2 reduce-scatter.16
  955.5 86.7 reduce-scatter.22
  1046.8 86.7 reduce-scatter.20
  1137.9 86.7 reduce-scatter.18
  1229.0 51.2 reduce-scatter.14
  1284.3 71.2 reduce-scatter.10
where the time goes:
time: 1370 us; the launch traced here: 1360 us
  waiting for transfers between devices  1060 us (77%)
  matrix products  172 us (13%)
  other arithmetic  54.6 us (4%)
  local copies, waits for them, and re-layouts  32.3 us (2%)
  blocking collectives  24.3 us (2%)
  between operations  16.5 us (1%)
    psum x1, waiting for transfers between devices, shards(): ffn_total = lax.psum(matmul(hidden, down_proj), 'tp')  218 us
    psum x1, waiting for transfers between devices, shards(): attn_total = lax.psum(matmul(context_flat, attn_out), 'tp')  155 us
    psum x1, waiting for transfers between devices, shards(): lax.psum(dot_cols(gate_delta, gate_proj) + dot_cols(up_delta, up_proj), '...  153 us
    reduce_scatter x1, waiting for transfers between devices, shards(): lax.psum_scatter(upproj_grad, 'seq', scatter_dimension=0, tiled=True)  91.3 us
    reduce_scatter x1, waiting for transfers between devices, shards(): lax.psum_scatter(down_grad, 'seq', scatter_dimension=1, tiled=True)  91.3 us
    reduce_scatter x1, waiting for transfers between devices, shards(): lax.psum_scatter(gate_grad, 'seq', scatter_dimension=0, tiled=True)  91.1 us
    reduce_scatter x1, waiting for transfers between devices, shards(): lax.psum_scatter(compress_grad, 'seq', scatter_dimension=0, tiled=True)  75.2 us
    reduce_scatter x1, waiting for transfers between devices, shards(): lax.psum_scatter(mixer_grad, 'seq', scatter_dimension=1, tiled=True)  62.4 us
  transfers between devices with their start and end apart: 12, of which 11 were waited for; matrix products, arithmetic and copies ran while one was open for 8% of the time, Pallas kernels for 0%

commit v1 on v0

--- a/solution.py
+++ b/solution.py
@@ -1,3 +1,4 @@
+import functools
 import jax
 import jax.numpy as jnp
 from jax import lax
@@ -7,6 +8,13 @@
 EPS = 1e-05
 ROPE_BASE = 10000.0
 NEG_FILL = -1e30
+
+
+def detail_group(chunk, shard_axis):
+    return lax.all_gather(chunk, shard_axis).sum(axis=0)
+
+
+press_wall = functools.partial(detail_group, shard_axis="tp")
 
 
 def matmul(left, right):
@@ -181,7 +189,7 @@
         .transpose(0, 2, 1, 3)
         .reshape(tokens, local_heads * HD)
     )
-    attn_total = lax.psum(matmul(context_flat, attn_out), "tp")
+    attn_total = press_wall(matmul(context_flat, attn_out))
     middle = stream + attn_total
     second_full, unit_second, inv_second = rms_forward(middle, ffn_gain)
     second_norm = second_full.astype(jnp.bfloat16)

time: 1370 us -> 1510 us (1.10)
  waiting for transfers between devices: 1060 us -> 1190 us
    all_gather x0 -> x1, waiting for transfers between devices: none -> 287 us  [detail_group(): return lax.all_gather(chunk, shard_axis).sum(axis=0)]
    psum x1 -> x0, waiting for transfers between devices: 155 us -> none  [shards(): attn_total = lax.psum(matmul(context_flat, attn_out), 'tp')]
where the time goes in v1:
time: 1510 us; the launch traced here: 1500 us
  waiting for transfers between devices  1190 us (79%)
  matrix products  171 us (11%)
  other arithmetic  68.5 us (5%)
  local copies, waits for them, and re-layouts  31.9 us (2%)
  blocking collectives  24.1 us (2%)
  between operations  16.5 us (1%)
    all_gather x1, waiting for transfers between devices, detail_group(): return lax.all_gather(chunk, shard_axis).sum(axis=0)  287 us
    psum x1, waiting for transfers between devices, shards(): ffn_total = lax.psum(matmul(hidden, down_proj), 'tp')  217 us
    psum x1, waiting for transfers between devices, shards(): lax.psum(dot_cols(gate_delta, gate_proj) + dot_cols(up_delta, up_proj), '...  153 us
    reduce_scatter x1, waiting for transfers between devices, shards(): lax.psum_scatter(upproj_grad, 'seq', scatter_dimension=0, tiled=True)  90.9 us
    reduce_scatter x1, waiting for transfers between devices, shards(): lax.psum_scatter(down_grad, 'seq', scatter_dimension=1, tiled=True)  90.9 us
    reduce_scatter x1, waiting for transfers between devices, shards(): lax.psum_scatter(gate_grad, 'seq', scatter_dimension=0, tiled=True)  90.7 us
    reduce_scatter x1, waiting for transfers between devices, shards(): lax.psum_scatter(compress_grad, 'seq', scatter_dimension=0, tiled=True)  75.6 us
    reduce_scatter x1, waiting for transfers between devices, shards(): lax.psum_scatter(mixer_grad, 'seq', scatter_dimension=1, tiled=True)  62.8 us
  transfers between devices with their start and end apart: 12, of which 11 were waited for; matrix products, arithmetic and copies ran while one was open for 8% of the time, Pallas kernels for 0%

profile of v1, /device:TPU:0, one launch (start us, length us, event | category | flops | bytes accessed | tf_op | source)
XLA Modules:
  0.0 1504.4 jit_solution(8583992302834394761)
XLA Ops:
  11.2 2.9 fusion.26
  23.6 2.6 fusion.65
  26.2 3.7 reshape.220
  33.8 2.7 iota_compare_fusion
  36.5 20.0 %all-gather.4.cloned.1.call-done = bf16[2,2048,512]{2,1,0:T(8,128)(2,1)} async-done(((bf16[2,256,512]{2,1,0:T(8,128)(2,1)}), bf16[2,2048,512]{2,1,0:T(8,128)(2,1)}) %all-gather.4.cloned.1.call-update) | async-done | bytes 4194320 | tf_op jit(solution)/shard_map/all_gather | solution.py:178
  56.5 7.5 fusion.66
  64.7 6.1 fusion
  70.8 8.2 fusion.42
  82.5 4.4 fusion.67
  86.9 286.9 %all-gather.6.cloned.1.call-done = f32[2048,2048]{1,0:T(8,128)} async-done(((f32[512,2048]{1,0:T(8,128)}), f32[2048,2048]{1,0:T(8,128)}) %all-gather.6.cloned.1.call-update) | async-done | bytes 16777232 | tf_op jit(solution)/shard_map/all_gather | solution.py:14
  373.8 10.2 reduce_sum.147
  383.9 3.6 fusion.24
  389.3 8.7 fusion.69
  398.2 4.9 fusion.68
  403.1 8.2 multiply_convert_fusion.2
  411.3 4.9 fusion.71
  416.3 5.1 convolution_add_fusion.1
  422.2 152.6 %all-reduce.8.cloned.1.call-done = f32[512,2048]{1,0:T(8,128)} async-done(((f32[512,2048]{1,0:T(8,128)}), f32[512,2048]{1,0:T(8,128)}) %all-reduce.8.cloned.1.call-update) | async-done | bytes 4194320 | tf_op jit(solution)/shard_map/psum | solution.py:213
  574.8 5.4 multiply_reduce_fusion
  581.9 3.4 multiply_add_fusion
  587.3 3.4 convolution_convert_fusion
  595.4 12.0 fusion.3
  607.5 13.8 multiply_convert_fusion
  621.3 6.9 convolution_multiply_fusion
  628.3 4.6 pad_maximum_fusion
  634.2 7.9 fusion.70
  642.2 7.2 fusion.36
  652.4 2.6 fusion.72
  655.0 48.4 %reduce-scatter.9.cloned.1.call-done = f32[2,256,512]{2,1,0:T(8,128)} async-done(((f32[2,2048,512]{2,1,0:T(8,128)}), f32[2,256,512]{2,1,0:T(8,128)}) %reduce-scatter.9.cloned.1.call-update) | async-done | bytes 1048592 | tf_op jit(solution)/shard_map/reduce_scatter | solution.py:238
  703.5 5.0 fusion.64
  709.7 8.1 fusion.39
  719.1 9.0 fusion.77
  729.4 7.9 fusion.76
  738.7 7.7 fusion.75
  746.5 217.4 %all-reduce.10.cloned.1.call-done = (f32[512,2048]{1,0:T(8,128)}, f32[512,1024]{1,0:T(8,128)}, f32[2,256,512]{2,1,0:T(8,128)}) async-done(((f32[512,2048]{1,0:T(8,128)}, f32[512,1024]{1,0:T(8,128)}, f32[2,256,512]{2,1,0:T(8,128)}), (f32[512,2048]{1,0:T(8,128)}, f32[512,1024]{1,0:T(8,128)}, f32[2,256,512]{2,1,0:T(8,128)})) %all-reduce.10.cloned.1.call-update) | async-done | bytes 7340048 | tf_op jit(solution)/shard_map/psum | solution.py:201
  967.8 4.9 fusion.58
  973.1 4.1 multiply_reduce_fusion.2
  978.3 5.7 fusion.74
  986.6 4.8 fusion.73
  991.5 3.8 fusion.19
  995.2 24.1 %all-reduce.3 = (f32[2048]{0:T(1024)S(1)}, f32[1024]{0:T(1024)S(1)}, f32[2048]{0:T(1024)S(1)}) all-reduce(f32[2048]{0:T(1024)S(1)} %get-tuple-element.14, f32[1024]{0:T(1024)S(1)} %copy-done.41, f32[2048]{0:T(1024)S(1)} %get-tuple-element.12), channel_id=4, replica_groups=mesh['seq'=8,'tp'=4] {'seq'}, use_global_device_ids=true, to_apply=%region_20.21.clone | all-reduce | flops 5120 | bytes 40960
  1021.2 9.9 fusion.18
  1031.1 62.8 %reduce-scatter.17.cloned.1.call-done = f32[1024,256]{1,0:T(8,128)} async-done(((f32[1024,2048]{1,0:T(8,128)}), f32[1024,256]{1,0:T(8,128)}) %reduce-scatter.17.cloned.1.call-update) | async-done | bytes 1048592 | tf_op jit(solution)/shard_map/reduce_scatter | solution.py:218
  1093.9 90.9 %reduce-scatter.23.cloned.1.call-done = f32[1408,256]{1,0:T(8,128)} async-done(((f32[1408,2048]{1,0:T(8,128)}), f32[1408,256]{1,0:T(8,128)}) %reduce-scatter.23.cloned.1.call-update) | async-done | bytes 1441808 | tf_op jit(solution)/shard_map/reduce_scatter | solution.py:219
  1184.8 90.9 %reduce-scatter.21.cloned.1.call-done = f32[256,1408]{1,0:T(8,128)} async-done(((f32[2048,1408]{1,0:T(8,128)}), f32[256,1408]{1,0:T(8,128)}) %reduce-scatter.21.cloned.1.call-update) | async-done | bytes 1441808 | tf_op jit(solution)/shard_map/reduce_scatter | solution.py:269
  1275.7 90.7 %reduce-scatter.19.cloned.1.call-done = f32[256,1408]{1,0:T(8,128)} async-done(((f32[2048,1408]{1,0:T(8,128)}), f32[256,1408]{1,0:T(8,128)}) %reduce-scatter.19.cloned.1.call-update) | async-done | bytes 1441808 | tf_op jit(solution)/shard_map/reduce_scatter | solution.py:268
  1366.4 55.3 %reduce-scatter.15.cloned.1.call-done = f32[256,512]{1,0:T(8,128)} async-done(((f32[2048,512]{1,0:T(8,128)}), f32[256,512]{1,0:T(8,128)}) %reduce-scatter.15.cloned.1.call-update) | async-done | bytes 524304 | tf_op jit(solution)/shard_map/reduce_scatter | solution.py:266
  1421.7 75.6 %reduce-scatter.11.cloned.1.call-done = f32[256,1024]{1,0:T(8,128)} async-done(((f32[2048,1024]{1,0:T(8,128)}), f32[256,1024]{1,0:T(8,128)}) %reduce-scatter.11.cloned.1.call-update) | async-done | bytes 1048592 | tf_op jit(solution)/shard_map/reduce_scatter | solution.py:263
  (200 shorter events, 50.2 us)
Async XLA Ops:
  7.2 49.3 %all-gather.4.cloned.1.call-start = ((), (), s32[]{:S(2)}) async-start(), calls=%async_computation.8 | async-start | bytes 4718592 | tf_op jit(solution)/shard_map/all_gather | solution.py:178
  7.3 6.9 copy-start.42
  9.1 5.1 copy-start.39
  11.2 5.8 copy-start.32
  16.0 13.9 copy-start.19
  16.9 356.8 %all-gather.6.cloned.1.call-start = ((), (), s32[]{:S(2)}) async-start(), calls=%async_computation.18 | async-start | bytes 20971520 | tf_op jit(solution)/shard_map/all_gather | solution.py:14
  17.0 5.3 copy-start.36
  56.5 8.1 copy-start.14
  64.1 6.7 copy-start.9
  86.8 487.9 %all-reduce.8.cloned.1.call-start = ((), (), s32[]{:S(2)}) async-start(), calls=%async_computation.9 | async-start | bytes 8388608 | tf_op jit(solution)/shard_map/psum | solution.py:213
  383.9 4.7 copy-start.3
  383.9 4.7 copy-start.29
  388.7 9.4 slice-start
  389.3 8.8 copy-start.22
  389.3 8.8 slice-start.1
  389.3 13.8 slice-start.4
  398.1 5.0 copy-start.21
  398.1 5.0 slice-start.5
  398.1 18.1 %slice-start.2 = ((s8[5767168]{0:T(1024)(128)(4,1)}), s8[4194304]{0:T(1024)(128)(4,1)S(1)}, s32[]{:S(2)}) async-start(s8[5767168]{0:T(1024)(128)(4,1)} %bitcast.158), calls=%async_computation.22 | async-start | bytes 8388608
  403.1 13.2 slice-start.3
  411.3 5.0 copy-start.54
  421.5 281.9 %reduce-scatter.9.cloned.1.call-start = ((), (), s32[]{:S(2)}) async-start(), calls=%async_computation.10 | async-start | bytes 9437184 | tf_op jit(solution)/shard_map/reduce_scatter | solution.py:238
  574.8 5.4 copy-start.2
  574.8 5.9 copy-start.4
  574.8 7.1 copy-start.10
  581.9 5.4 copy-start.45
  607.5 13.8 copy-start.24
  621.3 7.0 copy-start.16
  632.9 330.9 %all-reduce.10.cloned.1.call-start = ((), (), s32[]{:S(2)}) async-start(), calls=%async_computation.19 | async-start | bytes 14680064 | tf_op jit(solution)/shard_map/psum | solution.py:201
  634.2 7.9 copy-start.47
  655.0 48.5 %copy-start.28 = (f32[1024]{0:T(1024)S(1)}, f32[1024]{0:T(1024)}, u32[]{:S(2)}) copy-start(f32[1024]{0:T(1024)} %param.16) | copy-start | bytes 12292
  655.0 48.5 %copy-start.31 = (f32[512]{0:T(512)S(1)}, f32[512]{0:T(512)}, u32[]{:S(2)}) copy-start(f32[512]{0:T(512)} %copy-done.30) | copy-start | bytes 6148
  703.4 327.7 %reduce-scatter.13.cloned.1.call-start = ((), (), s32[]{:S(2)}) async-start(), calls=%async_computation.12 | async-start | bytes 4718592 | tf_op jit(solution)/shard_map/reduce_scatter | solution.py:265
  708.5 385.4 %reduce-scatter.17.cloned.1.call-start = ((), (), s32[]{:S(2)}) async-start(), calls=%async_computation.14 | async-start | bytes 9437184 | tf_op jit(solution)/shard_map/reduce_scatter | solution.py:218
  717.8 467.0 %reduce-scatter.23.cloned.1.call-start = ((), (), s32[]{:S(2)}) async-start(), calls=%async_computation.17 | async-start | bytes 12976128 | tf_op jit(solution)/shard_map/reduce_scatter | solution.py:219
  728.1 547.6 %reduce-scatter.21.cloned.1.call-start = ((), (), s32[]{:S(2)}) async-start(), calls=%async_computation.16 | async-start | bytes 12976128 | tf_op jit(solution)/shard_map/reduce_scatter | solution.py:269
  737.3 629.1 %reduce-scatter.19.cloned.1.call-start = ((), (), s32[]{:S(2)}) async-start(), calls=%async_computation.15 | async-start | bytes 12976128 | tf_op jit(solution)/shard_map/reduce_scatter | solution.py:268
  746.4 218.5 %copy-start.40 = (f32[2,256]{1,0:T(2,128)S(1)}, f32[2,256]{1,0:T(2,128)}, u32[]{:S(2)}) copy-start(f32[2,256]{1,0:T(2,128)} %copy-done.39) | copy-start | bytes 6148
  746.4 218.5 %copy-start.43 = (f32[128]{0:T(128)S(1)}, f32[128]{0:T(128)}, u32[]{:S(2)}) copy-start(f32[128]{0:T(128)} %copy-done.42) | copy-start | bytes 1540
  746.4 675.3 %reduce-scatter.15.cloned.1.call-start = ((), (), s32[]{:S(2)}) async-start(), calls=%async_computation.13 | async-start | bytes 4718592 | tf_op jit(solution)/shard_map/reduce_scatter | solution.py:266
  972.8 524.5 %reduce-scatter.11.cloned.1.call-start = ((), (), s32[]{:S(2)}) async-start(), calls=%async_computation.11 | async-start | bytes 9437184 | tf_op jit(solution)/shard_map/reduce_scatter | solution.py:263
  973.1 4.4 copy-start.13
  973.1 5.2 copy-start.12
  986.6 4.8 copy-start.5
  986.6 4.8 copy-start.26
  986.6 4.8 copy-start.33
  986.6 4.8 copy-start.37
  991.4 29.8 %copy-start.38 = (f32[1,2,2,128]{3,1,2,0:T(2,128)S(1)}, f32[1,2,2,128]{3,1,2,0:T(2,128)}, u32[]{:S(2)}) copy-start(f32[1,2,2,128]{3,1,2,0:T(2,128)} %copy-done.36) | copy-start | bytes 6148
  (26 other events, 53.9 us)
Sparse Core Ops, SparseCore 0:
  17.1 39.3 all-gather.3
  87.0 286.7 all-gather.5
  421.6 153.1 all-reduce.7
  633.0 70.2 reduce-scatter.8
  706.4 257.4 all-reduce.9
  967.6 50.4 reduce-scatter.12
  1022.6 71.2 reduce-scatter.16
  1098.0 86.7 reduce-scatter.22
  1188.9 86.7 reduce-scatter.20
  1279.6 86.7 reduce-scatter.18
  1370.4 51.3 reduce-scatter.14
  1426.0 71.2 reduce-scatter.10
